TPU v7x, 32 devices: a whole 2x2x4 slice. The times are simulated.
32 devices in a mesh: blk: 8 (over z, x), team: 4 (over y, core).
Axes of the slice: x: 2, y: 2, z: 4, core: 2. Of those that a mesh axis runs over, the one named last changes fastest.
Arguments:
- points: float32 [2048, 1024], P('blk'), may hold values from -80 to 80
- probes: float32 [2048, 256], P('blk'), may hold values from -6 to 6
Outputs:
- product: float32 [2048, 256], P(('blk', 'team'))
All inputs are finite; a program needn't handle non-finite values.
Results may differ from a plain program's by a relative error of at most 0.00014.
Values sent between devices are 32-bit elements; how exact they have to be, the bound alone decides.
A program may use at most 64 MiB of HBM per device.

v0:
```python
import jax
import jax.numpy as jnp
from jax import lax
from jax.sharding import PartitionSpec as P


def passed_along(value, axis, steps):
    count = lax.axis_size(axis)
    pairs = [(source, (source + steps) % count) for source in range(count)]
    return lax.ppermute(value, axis, pairs)


def kernel_block(own, own_sq, other, scale):
    other_sq = jnp.sum(other * other, axis=1)
    cross = lax.dot_general(
        own,
        other,
        (((1,), (1,)), ((), ())),
        precision=lax.Precision.HIGHEST,
        preferred_element_type=jnp.float32,
    )
    arg = (own_sq[:, None] + other_sq[None, :] - 2.0 * cross) * scale
    return jnp.exp(-jnp.maximum(arg, 0.0))


def body(points, probes):
    width = points.shape[1]
    probe_count = probes.shape[1]
    scale = 2.0 / width
    team = lax.axis_index("team")
    team_size = lax.axis_size("team")
    blocks = lax.axis_size("blk")
    own_sq = jnp.sum(points * points, axis=1)
    visitor = jnp.concatenate([points, probes], axis=1)
    for bit in range(team_size.bit_length() - 1):
        moved = passed_along(visitor, "blk", 1 << bit)
        visitor = jnp.where(team >> bit & 1 == 1, moved, visitor)
    total = jnp.zeros((points.shape[0], probe_count), jnp.float32)
    steps = blocks // team_size

    def accumulate(visitor, total):
        kernel = kernel_block(points, own_sq, visitor[:, :width], scale)
        return total + jnp.dot(
            kernel,
            visitor[:, width:],
            precision=lax.Precision.HIGHEST,
            preferred_element_type=jnp.float32,
        )

    def visit(step, carry):
        visitor, total = carry
        total = accumulate(visitor, total)
        visitor = passed_along(visitor, "blk", team_size)
        return (visitor, total)

    visitor, total = lax.fori_loop(0, steps - 1, visit, (visitor, total))
    total = accumulate(visitor, total)
    return lax.psum_scatter(total, "team", scatter_dimension=0, tiled=True)


def solution(mesh):
    in_specs = (P("blk", None), P("blk", None))
    out_specs = P(("blk", "team"), None)
    return jax.shard_map(body, mesh=mesh, in_specs=in_specs, out_specs=out_specs, check_vma=False)
```

profile of v0, /device:TPU:0, one launch (start us, length us, event | category | flops | bytes accessed | tf_op | source)
XLA Modules:
  0.0 161.7 jit_solution(4474935281150204840)
XLA Ops:
  6.5 0.0 copy-start.1
  6.5 0.0 reduce-scatter.2.cloned.1.call-start
  6.5 1.4 multiply_reduce_fusion.2
  8.0 0.0 copy-done.1
  8.0 3.0 %collective-permute-start = (f32[256,1280]{1,0:T(8,128)S(1)}, f32[256,1280]{1,0:T(8,128)}, u32[]{:S(2)}, u32[]{:S(2)}) collective-permute-start(f32[256,1280]{1,0:T(8,128)S(1)} %constant_dynamic-update-slice_fusion), channel_id=1, source_target_pairs={{0,4},{4,8},{8,12},{12,16},{16,20},{20,24},{24,28},{28,0},{1,5},{5... | collective-permute-start | bytes 3932168 | tf_op jit(solution)/shard_map/ppermute | solution.py:10
  11.0 31.9 %collective-permute-done = f32[256,1280]{1,0:T(8,128)} collective-permute-done((f32[256,1280]{1,0:T(8,128)S(1)}, f32[256,1280]{1,0:T(8,128)}, u32[]{:S(2)}, u32[]{:S(2)}) %collective-permute-start) | collective-permute-done | bytes 1310752 | tf_op jit(solution)/shard_map/ppermute | solution.py:10
  43.0 0.1 broadcast_select_fusion
  43.1 0.1 collective-permute-start.1
  43.2 33.0 %collective-permute-done.1 = f32[256,1280]{1,0:T(8,128)S(1)} collective-permute-done((f32[256,1280]{1,0:T(8,128)S(1)}, f32[256,1280]{1,0:T(8,128)S(1)}, u32[]{:S(2)}, u32[]{:S(2)}) %collective-permute-start.1) | collective-permute-done | bytes 1310752 | tf_op jit(solution)/shard_map/ppermute | solution.py:10
  76.2 0.1 broadcast_select_fusion.1
  76.4 0.0 copy-start
  76.4 0.1 collective-permute-start.2
  76.5 0.1 multiply_reduce_fusion.1
  76.6 1.0 copy-done
  77.6 1.1 fusion.6
  78.7 55.4 %collective-permute-done.2 = f32[256,1280]{1,0:T(8,128)S(1)} collective-permute-done((f32[256,1280]{1,0:T(8,128)S(1)}, f32[256,1280]{1,0:T(8,128)S(1)}, u32[]{:S(2)}, u32[]{:S(2)}) %collective-permute-start.2) | collective-permute-done | bytes 1310752 | tf_op jit(solution)/shard_map/while/body/eval_jaxpr/ppermute | solution.py:10
  134.0 0.1 multiply_reduce_fusion
  134.2 1.0 fusion
  135.2 0.4 fusion.9
  135.7 1.1 convolution_add_fusion
  136.7 0.0 reduce-scatter.2.cloned.1.call-update
  136.8 18.1 %reduce-scatter.2.cloned.1.call-done = f32[64,256]{1,0:T(8,128)} async-done(((f32[256,256]{1,0:T(8,128)}), f32[64,256]{1,0:T(8,128)}) %reduce-scatter.2.cloned.1.call-update) | async-done | bytes 65552 | tf_op jit(solution)/shard_map/reduce_scatter | solution.py:58
  (1 shorter events, 0.0 us)
Async XLA Ops:
  6.5 1.5 copy-start.1
  6.5 148.3 %reduce-scatter.2.cloned.1.call-start = ((), (), s32[]{:S(2)}) async-start(), calls=%async_computation.1 | async-start | bytes 327680 | tf_op jit(solution)/shard_map/reduce_scatter | solution.py:58
  8.0 34.9 %collective-permute-start = (f32[256,1280]{1,0:T(8,128)S(1)}, f32[256,1280]{1,0:T(8,128)}, u32[]{:S(2)}, u32[]{:S(2)}) collective-permute-start(f32[256,1280]{1,0:T(8,128)S(1)} %constant_dynamic-update-slice_fusion), channel_id=1, source_target_pairs={{0,4},{4,8},{8,12},{12,16},{16,20},{20,24},{24,28},{28,0},{1,5},{5... | collective-permute-start | bytes 3932168 | tf_op jit(solution)/shard_map/ppermute | solution.py:10
  43.1 33.1 %collective-permute-start.1 = (f32[256,1280]{1,0:T(8,128)S(1)}, f32[256,1280]{1,0:T(8,128)S(1)}, u32[]{:S(2)}, u32[]{:S(2)}) collective-permute-start(f32[256,1280]{1,0:T(8,128)S(1)} %broadcast_select_fusion), channel_id=1, source_target_pairs={{0,8},{4,12},{8,16},{12,20},{16,24},{20,28},{24,0},{28,4},{1,9},{5... | collective-permute-start | bytes 3932168 | tf_op jit(solution)/shard_map/ppermute | solution.py:10
  76.4 1.2 copy-start
  76.4 57.7 %collective-permute-start.2 = (f32[256,1280]{1,0:T(8,128)S(1)}, f32[256,1280]{1,0:T(8,128)S(1)}, u32[]{:S(2)}, u32[]{:S(2)}) collective-permute-start(f32[256,1280]{1,0:T(8,128)S(1)} %broadcast_select_fusion.1), channel_id=1, source_target_pairs={{0,16},{4,20},{8,24},{12,28},{16,0},{20,4},{24,8},{28,12},{1,17},{... | collective-permute-start | bytes 3932168 | tf_op jit(solution)/shard_map/while/body/eval_jaxpr/ppermute | solution.py:10
Sparse Core Ops, SparseCore 0:
  136.9 17.9 reduce-scatter.1
where the time goes:
time: 162 us
  waiting for transfers between devices  138 us (85%)
  between operations  13.5 us (8%)
  matrix products  3.61 us (2%)
  starting transfers between devices  3.15 us (2%)
  other arithmetic  2.04 us (1%)
    ppermute x3, waiting for transfers between devices, passed_along(): return lax.ppermute(value, axis, pairs)  120 us
    reduce_scatter x1, waiting for transfers between devices, body(): return lax.psum_scatter(total, 'team', scatter_dimension=0, tiled=True)  18.1 us
  transfers between devices with their start and end apart: 4, of which 4 were waited for; matrix products, arithmetic and copies ran while one was open for 1% of the time, Pallas kernels for 0%

commit v1 on v0

v1 whole, which is shorter than its diff:
```python
import functools

import jax
import jax.numpy as jnp
from jax import lax
from jax.experimental import pallas as pl
from jax.experimental.pallas import tpu as pltpu
from jax.sharding import PartitionSpec as P

HIGHEST = lax.Precision.HIGHEST
MESH = pl.DeviceIdType.MESH


def kernel(
    blocks,
    outer,
    inner,
    team_size,
    points_hbm,
    probes_hbm,
    out_ref,
    own,
    own_probes,
    all_points,
    all_probes,
    own_sq,
    total,
    parts,
    load_sem,
    recv_sem,
    extra_recv,
    send_outer,
    send_inner,
    extra_send,
    part_send,
    part_recv,
):
    rows, width = own.shape
    piece = rows // team_size
    half = piece // 2
    scale = 2.0 / width
    block = lax.axis_index("blk")
    team = lax.axis_index("team")
    z = block // inner
    x = lax.rem(block, inner)
    split = inner == 2 and outer > 2

    def at(layer, column):
        return layer * inner + column

    def rows_of(index, offset, count):
        return pl.ds(pl.multiple_of(index * piece + offset, half), count)

    def copy_pair(source, where, target, send, recv):
        made = []
        for which, (src, dst) in enumerate(((source[0], all_points), (source[1], all_probes))):
            made.append(
                pltpu.make_async_remote_copy(
                    src_ref=src,
                    dst_ref=dst.at[where],
                    send_sem=send.at[which],
                    recv_sem=recv.at[which],
                    device_id={"blk": target},
                    device_id_type=MESH,
                )
            )
        return made

    def gathered(where):
        return all_points.at[where], all_probes.at[where]

    own_rows = pl.ds(pl.multiple_of(team * piece, piece), piece)
    own_source = points_hbm.at[own_rows], probes_hbm.at[own_rows]

    def along_outer(layer, way, source=None):
        where = rows_of(at(layer, x), 0, piece)
        source = gathered(where) if source is None else source
        return copy_pair(
            source, where, at(z + way, x), send_outer.at[layer, (way + 1) // 2], recv_sem.at[at(layer, x)]
        )

    def along_inner(layer, step, count, source=None):
        where = rows_of(at(layer, x), 0, count)
        source = gathered(where) if source is None else source
        return copy_pair(
            source, where, at(z, lax.rem(x + step, inner)), send_inner.at[layer, step - 1], recv_sem.at[at(layer, x)]
        )

    def extra(end, way):
        layer = end * (outer - 1)
        where = rows_of(at(layer, 1 - x), half, half)
        return copy_pair(gathered(where), where, at(z + way, x), extra_send.at[end], extra_recv.at[end])

    def start(copies):
        for copy in copies:
            copy.start()

    def wait_send(copies):
        for copy in copies:
            copy.wait_send()

    def wait_recv(index, offset, count, sem):
        where = rows_of(index, offset, count)
        for which, dst in enumerate((all_points, all_probes)):
            pltpu.make_async_copy(dst.at[where], dst.at[where], sem.at[which]).wait()

    def is_end(layer):
        return (layer == 0) | (layer == outer - 1)

    def inside(layer):
        return (layer >= 0) & (layer < outer)

    def pair(visitor, visitor_probes):
        visitor_sq = jnp.sum(visitor * visitor, axis=1, keepdims=True)
        cross = lax.dot_general(
            visitor,
            own[...],
            (((1,), (1,)), ((), ())),
            precision=HIGHEST,
            preferred_element_type=jnp.float32,
        )
        arg = (visitor_sq + own_sq[...] - 2.0 * cross) * scale
        value = jnp.exp(-jnp.maximum(arg, 0.0))
        total[...] += jnp.dot(
            value.T, visitor_probes, precision=HIGHEST, preferred_element_type=jnp.float32
        )

    def pair_at(index, offset, count):
        where = rows_of(index, offset, count)
        pair(all_points[where, :], all_probes[where, :])

    barrier = pltpu.get_barrier_semaphore()
    for way in (1, -1):
        @pl.when(inside(z + way))
        def _(way=way):
            pl.semaphore_signal(barrier, inc=1, device_id={"blk": at(z + way, x)}, device_id_type=MESH)
    for step in range(1, inner):
        pl.semaphore_signal(
            barrier, inc=1, device_id={"blk": at(z, lax.rem(x + step, inner))}, device_id_type=MESH
        )
    for step in range(1, team_size):
        pl.semaphore_signal(
            barrier, inc=1, device_id={"team": lax.rem(team + step, team_size)}, device_id_type=MESH
        )
    loads = [
        pltpu.make_async_copy(points_hbm, own, load_sem.at[0]),
        pltpu.make_async_copy(probes_hbm, own_probes, load_sem.at[1]),
    ]
    start(loads)
    neighbours = jnp.where(z > 0, 1, 0) + jnp.where(z < outer - 1, 1, 0)
    pl.semaphore_wait(barrier, neighbours + inner - 1 + team_size - 1)

    for way in (1, -1):
        @pl.when(inside(z + way))
        def _(way=way):
            start(along_outer(z, way, own_source))
    for step in range(1, inner):
        start(along_inner(z, step, piece, own_source))

    for load in loads:
        load.wait()
    column = jnp.sum(own[...] * own[...], axis=1, keepdims=True)
    own_sq[...] = jnp.broadcast_to(column, (rows, 128)).T[0:1, :]
    total[...] = jnp.zeros_like(total)
    pair(own[own_rows, :], own_probes[own_rows, :])

    def from_inner(layer):
        for step in range(1, inner):
            index = at(layer, lax.rem(x + step, inner))
            if split:
                @pl.when(is_end(layer) & (layer != z))
                def _():
                    wait_recv(index, 0, half, recv_sem.at[index])
                    pair_at(index, 0, half)

                @pl.when(jnp.logical_not(is_end(layer) & (layer != z)))
                def _():
                    wait_recv(index, 0, piece, recv_sem.at[index])
            else:
                wait_recv(index, 0, piece, recv_sem.at[index])

    def pair_inner(layer):
        for step in range(1, inner):
            index = at(layer, lax.rem(x + step, inner))
            if split:
                @pl.when(jnp.logical_not(is_end(layer) & (layer != z)))
                def _():
                    pair_at(index, 0, piece)
            else:
                pair_at(index, 0, piece)

    def from_extra(layer, way):
        end = layer // (outer - 1)
        index = at(layer, 1 - x)
        wait_recv(index, half, half, extra_recv.at[end])

        @pl.when(inside(z - way))
        def _():
            start(extra(end, -way))
        pair_at(index, half, half)

    def arrive(k, carry):
        d = k // 2 + 1
        way = 1 - 2 * lax.rem(k, 2)
        layer = z + way * d

        @pl.when(inside(layer))
        def _():
            wait_recv(at(layer, x), 0, piece, recv_sem.at[at(layer, x)])

            @pl.when(inside(z - way))
            def _():
                start(along_outer(layer, -way))

            for step in range(1, inner):
                if split:
                    @pl.when(is_end(layer))
                    def _():
                        start(along_inner(layer, step, half))

                    @pl.when(jnp.logical_not(is_end(layer)))
                    def _():
                        start(along_inner(layer, step, piece))
                else:
                    start(along_inner(layer, step, piece))
            pair_at(at(layer, x), 0, piece)

        before = z + way * (d - 1)

        @pl.when(inside(before) & ((d > 1) | (way > 0)))
        def _():
            from_inner(before)
            if split:
                @pl.when((d == 1) & is_end(z))
                def _():
                    start(extra(z // (outer - 1), 1 - 2 * (z // (outer - 1))))
            pair_inner(before)
        if split:
            @pl.when(inside(before) & is_end(before) & (before != z))
            def _():
                from_extra(before, way)
        return carry

    lax.fori_loop(0, 2 * (outer - 1), arrive, 0)
    for way in (1, -1):
        last = z + way * (outer - 1)

        @pl.when(inside(last))
        def _(last=last, way=way):
            from_inner(last)
            pair_inner(last)
            if split:
                from_extra(last, way)

    def part(step):
        peer = lax.rem(team + step, team_size)
        return pltpu.make_async_remote_copy(
            src_ref=total.at[pl.ds(pl.multiple_of(peer * piece, piece), piece)],
            dst_ref=parts.at[step - 1],
            send_sem=part_send.at[step - 1],
            recv_sem=part_recv.at[step - 1],
            device_id={"team": peer},
            device_id_type=MESH,
        )

    for step in range(1, team_size):
        part(step).start()
    for way in (1, -1):
        @pl.when(inside(z + way))
        def _(way=way):
            wait_send(along_outer(z, way, own_source))
    for step in range(1, inner):
        wait_send(along_inner(z, step, piece, own_source))

    def sent(k, carry):
        d = k // 2 + 1
        way = 1 - 2 * lax.rem(k, 2)
        layer = z + way * d

        @pl.when(inside(layer))
        def _():
            @pl.when(inside(z - way))
            def _():
                wait_send(along_outer(layer, -way))

            for step in range(1, inner):
                if split:
                    @pl.when(is_end(layer))
                    def _():
                        wait_send(along_inner(layer, step, half))

                    @pl.when(jnp.logical_not(is_end(layer)))
                    def _():
                        wait_send(along_inner(layer, step, piece))
                else:
                    wait_send(along_inner(layer, step, piece))
            if split:
                @pl.when(is_end(layer) & inside(z - way))
                def _():
                    wait_send(extra(layer // (outer - 1), -way))
        return carry

    lax.fori_loop(0, 2 * (outer - 1), sent, 0)
    if split:
        @pl.when(is_end(z))
        def _():
            wait_send(extra(z // (outer - 1), 1 - 2 * (z // (outer - 1))))
    result = total[own_rows, :]
    for step in range(1, team_size):
        part(step).wait_recv()
        result = result + parts[step - 1]
    out_ref[...] = result
    for step in range(1, team_size):
        part(step).wait_send()


def body(points, probes):
    rows, width = points.shape
    count = probes.shape[1]
    team_size = lax.axis_size("team")
    blocks = lax.axis_size("blk")
    inner = 1 << ((blocks.bit_length() - 1) // 2)
    outer = blocks // inner
    piece = rows // team_size
    f32 = jnp.float32
    dma = pltpu.SemaphoreType.DMA
    return pl.pallas_call(
        functools.partial(kernel, blocks, outer, inner, team_size),
        out_shape=jax.ShapeDtypeStruct((piece, count), f32),
        in_specs=[pl.BlockSpec(memory_space=pl.ANY)] * 2,
        out_specs=pl.BlockSpec(memory_space=pltpu.VMEM),
        scratch_shapes=[
            pltpu.VMEM((rows, width), f32),
            pltpu.VMEM((rows, count), f32),
            pltpu.VMEM((blocks * piece, width), f32),
            pltpu.VMEM((blocks * piece, count), f32),
            pltpu.VMEM((1, rows), f32),
            pltpu.VMEM((rows, count), f32),
            pltpu.VMEM((team_size - 1, piece, count), f32),
            dma((2,)),
            dma((blocks, 2)),
            dma((2, 2)),
            dma((outer, 2, 2)),
            dma((outer, max(inner - 1, 1), 2)),
            dma((2, 2)),
            dma((team_size - 1,)),
            dma((team_size - 1,)),
        ],
        compiler_params=pltpu.CompilerParams(collective_id=0, has_side_effects=True),
    )(points, probes)


def solution(mesh):
    in_specs = (P("blk", None), P("blk", None))
    out_specs = P(("blk", "team"), None)
    return jax.shard_map(body, mesh=mesh, in_specs=in_specs, out_specs=out_specs, check_vma=False)
```

time: 162 us -> 45.5 us (0.28)
  the two profiles are of different devices: /device:TPU:0 before, /device:TPU:29 now
where the time goes in v1:
time: 45.5 us; the launch traced here: 45.3 us
  Pallas kernels  43.9 us (96%)
  local copies, waits for them, and re-layouts  1.47 us (3%)
    pallas_call x1, Pallas kernels, body(): pl.pallas_call(functools.partial(kernel, blocks, outer, inner, team_size)...  43.9 us
    unnamed x1, local copies, waits for them, and re-layouts  1.47 us

profile of v1, /device:TPU:29, one launch (start us, length us, event | category | flops | bytes accessed | tf_op | source)
XLA Modules:
  0.0 45.3 jit_solution(5345254597357384996)
XLA Ops:
  0.0 43.9 %shard_map.28 = f32[64,256]{1,0:T(8,128)} custom-call(f32[256,1024]{1,0:T(8,128)} %points_hbm.1, f32[256,256]{1,0:T(8,128)} %probes_hbm.1), custom_call_target="tpu_custom_call" | custom-call | tf_op jit(solution)/shard_map/pallas_call | solution.py:327
  43.9 1.5 %copy.4 = f32[64,256]{1,0:T(8,128)} copy(f32[64,256]{1,0:T(8,128)} %shard_map.28) | data formatting | bytes 131072

commit v2 on v0

v2 whole, which is shorter than its diff:
```python
import functools

import jax
import jax.numpy as jnp
from jax import lax
from jax.experimental import pallas as pl
from jax.experimental.pallas import tpu as pltpu
from jax.sharding import PartitionSpec as P

HIGHEST = lax.Precision.HIGHEST
MESH = pl.DeviceIdType.MESH


def kernel(
    outer,
    inner,
    points_hbm,
    probes_hbm,
    out_ref,
    layer_points,
    layer_probes,
    layer_sq,
    visitors,
    sums,
    returned,
    load_sem,
    visit_send,
    visit_recv,
    row_send,
    share_send,
    row_recv,
    back_send,
    back_recv,
):
    rows, width = points_hbm.shape
    piece = visitors.shape[1]
    half = rows // 2
    sub = half // 2
    scale = 2.0 / width
    block = lax.axis_index("blk")
    team = lax.axis_index("team")
    z = block // inner
    x = lax.rem(block, inner)
    core = lax.rem(team, 2)
    sibling = {"team": team + 1 - 2 * core}

    def at(layer, column):
        return {"blk": layer * inner + column}

    def inside(layer):
        return (layer >= 0) & (layer < outer)

    def remote(src, dst, send, recv, target):
        return pltpu.make_async_remote_copy(
            src_ref=src, dst_ref=dst, send_sem=send, recv_sem=recv, device_id=target, device_id_type=MESH
        )

    def wait_recv(ref, sem):
        pltpu.make_async_copy(ref, ref, sem).wait()

    own_rows = pl.ds(pl.multiple_of(team * piece, piece), piece)

    def onward(layer, way, source=None):
        return remote(
            visitors.at[layer] if source is None else source,
            visitors.at[layer],
            visit_send.at[layer, (way + 1) // 2],
            visit_recv.at[layer],
            at(z + way, x),
        )

    def slot(column, part, side):
        return (column * 2 + part) * 2 + side

    def slot_rows(column, part, side):
        return pl.ds(pl.multiple_of(column * rows + part * half + side * sub, sub), sub)

    def across(step, part):
        source = pl.ds(pl.multiple_of(part * half + core * sub, sub), sub)
        where = slot_rows(x, part, core)
        return [
            remote(
                src.at[source],
                dst.at[where],
                row_send.at[step - 1, part, which],
                row_recv.at[slot(x, part, core), which],
                at(z, lax.rem(x + step, inner)),
            )
            for which, (src, dst) in enumerate(((points_hbm, layer_points), (probes_hbm, layer_probes)))
        ]

    def share(step, part):
        column = lax.rem(x + step, inner)
        where = slot_rows(column, part, core)
        return [
            remote(
                ref.at[where],
                ref.at[where],
                share_send.at[step - 1, part, which],
                row_recv.at[slot(column, part, core), which],
                sibling,
            )
            for which, ref in enumerate((layer_points, layer_probes))
        ]

    def wait_rows(column, part, side):
        for which, ref in enumerate((layer_points, layer_probes)):
            wait_recv(ref.at[slot_rows(column, part, side)], row_recv.at[slot(column, part, side), which])

    def back(layer):
        return remote(sums.at[layer], returned.at[z], back_send.at[layer], back_recv.at[z], at(layer, x))

    def half_rows(column, part):
        return pl.ds(pl.multiple_of(column * rows + part * half, half), half)

    def square(column, part):
        values = layer_points[half_rows(column, part), :]
        total = jnp.sum(values * values, axis=1, keepdims=True)
        layer_sq[column * 2 + part] = jnp.broadcast_to(total, (half, 128)).T[0:1, :]

    def pair(layer, column, parts, fresh=False):
        first = parts[0]
        where = pl.ds(pl.multiple_of(column * rows + first * half, half), half * len(parts))
        visitor = visitors[layer]
        visitor_sq = jnp.sum(visitor * visitor, axis=1, keepdims=True)
        cross = lax.dot_general(
            visitor,
            layer_points[where, :],
            (((1,), (1,)), ((), ())),
            precision=HIGHEST,
            preferred_element_type=jnp.float32,
        )
        row_sq = jnp.concatenate([layer_sq[column * 2 + part] for part in parts], axis=1)
        arg = (visitor_sq + row_sq - 2.0 * cross) * scale
        value = jnp.exp(-jnp.maximum(arg, 0.0))
        product = jnp.dot(
            value, layer_probes[where, :], precision=HIGHEST, preferred_element_type=jnp.float32
        )
        sums[layer] = product if fresh else sums[layer] + product

    barrier = pltpu.get_barrier_semaphore()
    for step in range(1, outer):
        pl.semaphore_signal(barrier, inc=1, device_id=at(lax.rem(z + step, outer), x), device_id_type=MESH)
    for step in range(1, inner):
        pl.semaphore_signal(barrier, inc=1, device_id=at(z, lax.rem(x + step, inner)), device_id_type=MESH)
    pl.semaphore_signal(barrier, inc=1, device_id=sibling, device_id_type=MESH)
    mine = pl.ds(pl.multiple_of(x * rows, rows), rows)
    loads = [
        pltpu.make_async_copy(points_hbm, layer_points.at[mine], load_sem.at[0]),
        pltpu.make_async_copy(probes_hbm, layer_probes.at[mine], load_sem.at[1]),
        pltpu.make_async_copy(points_hbm.at[own_rows], visitors.at[z], load_sem.at[2]),
    ]
    for load in loads:
        load.start()
    pl.semaphore_wait(barrier, outer - 1 + inner - 1 + 1)

    for way in (1, -1):
        @pl.when(inside(z + way))
        def _(way=way):
            onward(z, way, points_hbm.at[own_rows]).start()
    for part in range(2):
        for step in range(1, inner):
            for copy in across(step, part):
                copy.start()

    for load in loads:
        load.wait()
    square(x, 0)
    square(x, 1)
    pair(z, x, (0, 1), fresh=True)

    def both_ways(distance, work):
        def one(k, carry):
            layer = z + (1 - 2 * k) * distance

            @pl.when(inside(layer))
            def _():
                work(layer, 1 - 2 * k)
            return carry
        lax.fori_loop(0, 2, one, 0)

    def receive(layer, way):
        wait_recv(visitors.at[layer], visit_recv.at[layer])

        @pl.when(inside(z - way))
        def _():
            onward(layer, -way).start()
        pair(layer, x, (0, 1), fresh=True)

    def others(work):
        def one(step, carry):
            work(step, lax.rem(x + step, inner))
            return carry
        lax.fori_loop(1, inner, one, 0)

    def take_rows(part, reach):
        def take(step, column):
            wait_rows(column, part, core)
            for copy in share(step, part):
                copy.start()
        others(take)

        def use(step, column):
            wait_rows(column, part, 1 - core)
            square(column, part)

            def one(k, carry):
                layer = z + k - reach

                @pl.when(inside(layer))
                def _():
                    pair(layer, column, (part,))
                return carry
            lax.fori_loop(0, 2 * reach + 1, one, 0)
        others(use)

    near = min(2, outer - 1)
    both_ways(1, receive)
    take_rows(0, 1)
    if near == 2:
        def receive_more(layer, way):
            receive(layer, way)
            others(lambda step, column: pair(layer, column, (0,)))
        both_ways(2, receive_more)
    take_rows(1, near)
    for distance in range(1, near + 1):
        both_ways(distance, lambda layer, way: back(layer).start())

    def receive_all(layer, way):
        receive(layer, way)
        others(lambda step, column: pair(layer, column, (0, 1)))
        back(layer).start()
    for distance in range(near + 1, outer):
        both_ways(distance, receive_all)

    for way in (1, -1):
        @pl.when(inside(z + way))
        def _(way=way):
            onward(z, way, points_hbm.at[own_rows]).wait_send()

    def sent(layer, way):
        @pl.when(inside(z - way))
        def _():
            onward(layer, -way).wait_send()
    for distance in range(1, outer):
        both_ways(distance, sent)
    for part in range(2):
        for step in range(1, inner):
            for copy in across(step, part) + share(step, part):
                copy.wait_send()

    result = sums[z]
    for step in range(1, outer):
        layer = lax.rem(z + step, outer)
        wait_recv(returned.at[layer], back_recv.at[layer])
        result = result + returned[layer]
    out_ref[...] = result
    for step in range(1, outer):
        back(lax.rem(z + step, outer)).wait_send()


def body(points, probes):
    rows, width = points.shape
    count = probes.shape[1]
    blocks = lax.axis_size("blk")
    inner = 1 << ((blocks.bit_length() - 1) // 2)
    outer = blocks // inner
    piece = rows // lax.axis_size("team")
    f32 = jnp.float32
    dma = pltpu.SemaphoreType.DMA
    return pl.pallas_call(
        functools.partial(kernel, outer, inner),
        out_shape=jax.ShapeDtypeStruct((piece, count), f32),
        in_specs=[pl.BlockSpec(memory_space=pl.ANY)] * 2,
        out_specs=pl.BlockSpec(memory_space=pltpu.VMEM),
        scratch_shapes=[
            pltpu.VMEM((inner * rows, width), f32),
            pltpu.VMEM((inner * rows, count), f32),
            pltpu.VMEM((inner * 2, 1, rows // 2), f32),
            pltpu.VMEM((outer, piece, width), f32),
            pltpu.VMEM((outer, piece, count), f32),
            pltpu.VMEM((outer, piece, count), f32),
            dma((3,)),
            dma((outer, 2)),
            dma((outer,)),
            dma((inner - 1, 2, 2)),
            dma((inner - 1, 2, 2)),
            dma((inner * 4, 2)),
            dma((outer,)),
            dma((outer,)),
        ],
        compiler_params=pltpu.CompilerParams(collective_id=0, has_side_effects=True),
    )(points, probes)


def solution(mesh):
    in_specs = (P("blk", None), P("blk", None))
    out_specs = P(("blk", "team"), None)
    return jax.shard_map(body, mesh=mesh, in_specs=in_specs, out_specs=out_specs, check_vma=False)
```

time: 162 us -> 38.2 us (0.24)
  waiting for transfers between devices: 138 us -> 0 us
  Pallas kernels: 0 us -> 36.6 us
  between operations: 13.5 us -> 0.01 us
  matrix products: 3.61 us -> 0 us
  starting transfers between devices: 3.15 us -> 0 us
  other arithmetic: 2.04 us -> 0 us
    ppermute x3 -> x0, waiting for transfers between devices: 120 us -> none  [passed_along(): return lax.ppermute(value, axis, pairs)]
    pallas_call x0 -> x1, Pallas kernels: none -> 36.6 us  [body(): pl.pallas_call(functools.partial(kernel, outer, inner), out_shape=jax.Sha...]
    reduce_scatter x1 -> x0, waiting for transfers between devices: 18.1 us -> none  [body(): return lax.psum_scatter(total, 'team', scatter_dimension=0, tiled=True)]
    dot_general x4 -> x0, matrix products: 3.61 us -> none  [the longest x2 2.09 us: kernel_block(): lax.dot_general(own, other, (((1,), (1,)), ((), ())), precision=lax.Preci...]
    ppermute x3 -> x0, starting transfers between devices: 3.15 us -> none  [passed_along(): return lax.ppermute(value, axis, pairs)]
    reduce_sum x3 -> x0, other arithmetic: 1.74 us -> none  [the longest x1 1.45 us: body(): own_sq = jnp.sum(points * points, axis=1)]
  transfers between devices with their start and end apart: 4 -> 0, of which waited for: 4 -> 0; matrix products, arithmetic and copies ran while one was open for 1% -> 0% of each run, Pallas kernels for 0% -> 0%
where the time goes in v2:
time: 38.2 us; the launch traced here: 38.1 us
  Pallas kernels  36.6 us (96%)
  local copies, waits for them, and re-layouts  1.47 us (4%)
    pallas_call x1, Pallas kernels, body(): pl.pallas_call(functools.partial(kernel, outer, inner), out_shape=jax.Sha...  36.6 us
    unnamed x1, local copies, waits for them, and re-layouts  1.47 us

profile of v2, /device:TPU:0, one launch (start us, length us, event | category | flops | bytes accessed | tf_op | source)
XLA Modules:
  0.0 38.1 jit_solution(4595801833632457655)
XLA Ops:
  0.0 36.6 %shard_map.28 = f32[64,256]{1,0:T(8,128)} custom-call(f32[256,1024]{1,0:T(8,128)} %points_hbm.1, f32[256,256]{1,0:T(8,128)} %probes_hbm.1), custom_call_target="tpu_custom_call" | custom-call | tf_op jit(solution)/shard_map/pallas_call | solution.py:271
  36.6 1.5 %copy.4 = f32[64,256]{1,0:T(8,128)} copy(f32[64,256]{1,0:T(8,128)} %shard_map.28) | data formatting | bytes 131072

commit v3 on v2

--- a/solution.py
+++ b/solution.py
@@ -7,7 +7,6 @@
 from jax.experimental.pallas import tpu as pltpu
 from jax.sharding import PartitionSpec as P
 
-HIGHEST = lax.Precision.HIGHEST
 MESH = pl.DeviceIdType.MESH
 
 
@@ -19,8 +18,14 @@
     out_ref,
     layer_points,
     layer_probes,
+    points_high,
+    points_low,
+    probes_high,
+    probes_low,
     layer_sq,
     visitors,
+    visitor_terms,
+    visitor_sq,
     sums,
     returned,
     load_sem,
@@ -60,12 +65,15 @@
 
     own_rows = pl.ds(pl.multiple_of(team * piece, piece), piece)
 
-    def onward(layer, way, source=None):
+    def onward(layer, way, turn, first=False):
+        where = pl.ds(turn * (piece // 2), piece // 2)
         return remote(
-            visitors.at[layer] if source is None else source,
-            visitors.at[layer],
-            visit_send.at[layer, (way + 1) // 2],
-            visit_recv.at[layer],
+            points_hbm.at[pl.ds(pl.multiple_of(team * piece + turn * (piece // 2), piece // 2), piece // 2)]
+            if first
+            else visitors.at[layer, where],
+            visitors.at[layer, where],
+            visit_send.at[layer, (way + 1) // 2, turn],
+            visit_recv.at[layer, turn],
             at(z + way, x),
         )
 
@@ -113,28 +121,49 @@
     def half_rows(column, part):
         return pl.ds(pl.multiple_of(column * rows + part * half, half), half)
 
-    def square(column, part):
-        values = layer_points[half_rows(column, part), :]
+    def two_terms(values):
+        high = values.astype(jnp.bfloat16)
+        return high, (values - high.astype(jnp.float32)).astype(jnp.bfloat16)
+
+    def four_products(stacked, high, low, contract):
+        count = stacked.shape[0] // 2
+        dot = functools.partial(
+            lax.dot_general,
+            dimension_numbers=(contract, ((), ())),
+            preferred_element_type=jnp.float32,
+        )
+        by_high, by_low = dot(stacked, high), dot(stacked, low)
+        return by_high[:count] + (by_high[count:] + by_low[:count] + by_low[count:])
+
+    def prepare_rows(column, part):
+        where = half_rows(column, part)
+        values = layer_points[where, :]
         total = jnp.sum(values * values, axis=1, keepdims=True)
         layer_sq[column * 2 + part] = jnp.broadcast_to(total, (half, 128)).T[0:1, :]
+        points_high[where, :], points_low[where, :] = two_terms(values)
+        probes_high[where, :], probes_low[where, :] = two_terms(layer_probes[where, :])
+
+    def prepare_visitor(layer):
+        values = visitors[layer]
+        visitor_sq[layer] = jnp.sum(values * values, axis=1, keepdims=True)
+        high, low = two_terms(values)
+        visitor_terms[layer, 0:piece, :] = high
+        visitor_terms[layer, piece : 2 * piece, :] = low
 
     def pair(layer, column, parts, fresh=False):
         first = parts[0]
         where = pl.ds(pl.multiple_of(column * rows + first * half, half), half * len(parts))
-        visitor = visitors[layer]
-        visitor_sq = jnp.sum(visitor * visitor, axis=1, keepdims=True)
-        cross = lax.dot_general(
-            visitor,
-            layer_points[where, :],
-            (((1,), (1,)), ((), ())),
-            precision=HIGHEST,
-            preferred_element_type=jnp.float32,
+        cross = four_products(
+            visitor_terms[layer], points_high[where, :], points_low[where, :], ((1,), (1,))
         )
         row_sq = jnp.concatenate([layer_sq[column * 2 + part] for part in parts], axis=1)
-        arg = (visitor_sq + row_sq - 2.0 * cross) * scale
+        arg = (visitor_sq[layer] + row_sq - 2.0 * cross) * scale
         value = jnp.exp(-jnp.maximum(arg, 0.0))
-        product = jnp.dot(
-            value, layer_probes[where, :], precision=HIGHEST, preferred_element_type=jnp.float32
+        product = four_products(
+            jnp.concatenate(two_terms(value), axis=0),
+            probes_high[where, :],
+            probes_low[where, :],
+            ((1,), (0,)),
         )
         sums[layer] = product if fresh else sums[layer] + product
 
@@ -157,7 +186,8 @@
     for way in (1, -1):
         @pl.when(inside(z + way))
         def _(way=way):
-            onward(z, way, points_hbm.at[own_rows]).start()
+            onward(z, way, 0, first=True).start()
+            onward(z, way, 1, first=True).start()
     for part in range(2):
         for step in range(1, inner):
             for copy in across(step, part):
@@ -165,8 +195,9 @@
 
     for load in loads:
         load.wait()
-    square(x, 0)
-    square(x, 1)
+    prepare_rows(x, 0)
+    prepare_rows(x, 1)
+    prepare_visitor(z)
     pair(z, x, (0, 1), fresh=True)
 
     def both_ways(distance, work):
@@ -179,13 +210,14 @@
             return carry
         lax.fori_loop(0, 2, one, 0)
 
-    def receive(layer, way):
-        wait_recv(visitors.at[layer], visit_recv.at[layer])
-
-        @pl.when(inside(z - way))
-        def _():
-            onward(layer, -way).start()
-        pair(layer, x, (0, 1), fresh=True)
+    def receive(distance, turn):
+        def work(layer, way):
+            wait_recv(visitors.at[layer, pl.ds(turn * (piece // 2), piece // 2)], visit_recv.at[layer, turn])
+
+            @pl.when(inside(z - way))
+            def _():
+                onward(layer, -way, turn).start()
+        both_ways(distance, work)
 
     def others(work):
         def one(step, carry):
@@ -193,16 +225,17 @@
             return carry
         lax.fori_loop(1, inner, one, 0)
 
-    def take_rows(part, reach):
+    def take_rows(part):
         def take(step, column):
             wait_rows(column, part, core)
             for copy in share(step, part):
                 copy.start()
         others(take)
 
+    def use_rows(part, reach):
         def use(step, column):
             wait_rows(column, part, 1 - core)
-            square(column, part)
+            prepare_rows(column, part)
 
             def one(k, carry):
                 layer = z + k - reach
@@ -214,34 +247,50 @@
             lax.fori_loop(0, 2 * reach + 1, one, 0)
         others(use)
 
+    def meet_own(layer, way):
+        prepare_visitor(layer)
+        pair(layer, x, (0, 1), fresh=True)
+
     near = min(2, outer - 1)
-    both_ways(1, receive)
-    take_rows(0, 1)
+    receive(1, 0)
+    receive(1, 1)
+    both_ways(1, meet_own)
+    take_rows(0)
     if near == 2:
-        def receive_more(layer, way):
-            receive(layer, way)
+        receive(2, 0)
+    use_rows(0, 1)
+    if near == 2:
+        receive(2, 1)
+
+        def meet_more(layer, way):
+            meet_own(layer, way)
             others(lambda step, column: pair(layer, column, (0,)))
-        both_ways(2, receive_more)
-    take_rows(1, near)
+        both_ways(2, meet_more)
+    take_rows(1)
+    use_rows(1, near)
     for distance in range(1, near + 1):
         both_ways(distance, lambda layer, way: back(layer).start())
 
-    def receive_all(layer, way):
-        receive(layer, way)
+    def meet_all(layer, way):
+        meet_own(layer, way)
         others(lambda step, column: pair(layer, column, (0, 1)))
         back(layer).start()
     for distance in range(near + 1, outer):
-        both_ways(distance, receive_all)
+        receive(distance, 0)
+        receive(distance, 1)
+        both_ways(distance, meet_all)
 
     for way in (1, -1):
         @pl.when(inside(z + way))
         def _(way=way):
-            onward(z, way, points_hbm.at[own_rows]).wait_send()
+            onward(z, way, 0, first=True).wait_send()
+            onward(z, way, 1, first=True).wait_send()
 
     def sent(layer, way):
         @pl.when(inside(z - way))
         def _():
-            onward(layer, -way).wait_send()
+            onward(layer, -way, 0).wait_send()
+            onward(layer, -way, 1).wait_send()
     for distance in range(1, outer):
         both_ways(distance, sent)
     for part in range(2):
@@ -266,7 +315,7 @@
     inner = 1 << ((blocks.bit_length() - 1) // 2)
     outer = blocks // inner
     piece = rows // lax.axis_size("team")
-    f32 = jnp.float32
+    f32, bf16 = jnp.float32, jnp.bfloat16
     dma = pltpu.SemaphoreType.DMA
     return pl.pallas_call(
         functools.partial(kernel, outer, inner),
@@ -276,13 +325,19 @@
         scratch_shapes=[
             pltpu.VMEM((inner * rows, width), f32),
             pltpu.VMEM((inner * rows, count), f32),
+            pltpu.VMEM((inner * rows, width), bf16),
+            pltpu.VMEM((inner * rows, width), bf16),
+            pltpu.VMEM((inner * rows, count), bf16),
+            pltpu.VMEM((inner * rows, count), bf16),
             pltpu.VMEM((inner * 2, 1, rows // 2), f32),
             pltpu.VMEM((outer, piece, width), f32),
+            pltpu.VMEM((outer, 2 * piece, width), bf16),
+            pltpu.VMEM((outer, piece, 1), f32),
             pltpu.VMEM((outer, piece, count), f32),
             pltpu.VMEM((outer, piece, count), f32),
             dma((3,)),
+            dma((outer, 2, 2)),
             dma((outer, 2)),
-            dma((outer,)),
             dma((inner - 1, 2, 2)),
             dma((inner - 1, 2, 2)),
             dma((inner * 4, 2)),

time: 38.2 us -> 33.6 us (0.88)
  Pallas kernels: 36.6 us -> 31.8 us
    pallas_call x1, Pallas kernels: 36.6 us -> 31.8 us  [body(): pl.pallas_call(functools.partial(kernel, outer, inner), out_shape=jax.Sha...]
where the time goes in v3:
time: 33.6 us; the launch traced here: 33.3 us
  Pallas kernels  31.8 us (95%)
  local copies, waits for them, and re-layouts  1.47 us (4%)
    pallas_call x1, Pallas kernels, body(): pl.pallas_call(functools.partial(kernel, outer, inner), out_shape=jax.Sha...  31.8 us
    unnamed x1, local copies, waits for them, and re-layouts  1.47 us

profile of v3, /device:TPU:0, one launch (start us, length us, event | category | flops | bytes accessed | tf_op | source)
XLA Modules:
  0.0 33.3 jit_solution(4383251204605251636)
XLA Ops:
  0.0 31.8 %shard_map.28 = f32[64,256]{1,0:T(8,128)} custom-call(f32[256,1024]{1,0:T(8,128)} %points_hbm.1, f32[256,256]{1,0:T(8,128)} %probes_hbm.1), custom_call_target="tpu_custom_call" | custom-call | tf_op jit(solution)/shard_map/pallas_call | solution.py:320
  31.8 1.5 %copy.4 = f32[64,256]{1,0:T(8,128)} copy(f32[64,256]{1,0:T(8,128)} %shard_map.28) | data formatting | bytes 131072

commit v4 on v3

--- a/solution.py
+++ b/solution.py
@@ -115,8 +115,15 @@
         for which, ref in enumerate((layer_points, layer_probes)):
             wait_recv(ref.at[slot_rows(column, part, side)], row_recv.at[slot(column, part, side), which])
 
-    def back(layer):
-        return remote(sums.at[layer], returned.at[z], back_send.at[layer], back_recv.at[z], at(layer, x))
+    def back(layer, turn):
+        where = pl.ds(turn * (piece // 2), piece // 2)
+        return remote(
+            sums.at[layer, where],
+            returned.at[z, where],
+            back_send.at[layer, turn],
+            back_recv.at[z, turn],
+            at(layer, x),
+        )
 
     def half_rows(column, part):
         return pl.ds(pl.multiple_of(column * rows + part * half, half), half)
@@ -143,21 +150,30 @@
         points_high[where, :], points_low[where, :] = two_terms(values)
         probes_high[where, :], probes_low[where, :] = two_terms(layer_probes[where, :])
 
-    def prepare_visitor(layer):
-        values = visitors[layer]
-        visitor_sq[layer] = jnp.sum(values * values, axis=1, keepdims=True)
+    def prepare_visitor(layer, begin=0, count=piece):
+        values = visitors[layer, begin : begin + count, :]
+        visitor_sq[layer, begin : begin + count] = jnp.sum(values * values, axis=1, keepdims=True)
         high, low = two_terms(values)
-        visitor_terms[layer, 0:piece, :] = high
-        visitor_terms[layer, piece : 2 * piece, :] = low
-
-    def pair(layer, column, parts, fresh=False):
+        visitor_terms[layer, begin : begin + count, :] = high
+        visitor_terms[layer, piece + begin : piece + begin + count, :] = low
+
+    def pair(layer, column, parts, fresh=False, begin=0, count=piece):
         first = parts[0]
         where = pl.ds(pl.multiple_of(column * rows + first * half, half), half * len(parts))
         cross = four_products(
-            visitor_terms[layer], points_high[where, :], points_low[where, :], ((1,), (1,))
+            jnp.concatenate(
+                [
+                    visitor_terms[layer, begin : begin + count, :],
+                    visitor_terms[layer, piece + begin : piece + begin + count, :],
+                ],
+                axis=0,
+            ),
+            points_high[where, :],
+            points_low[where, :],
+            ((1,), (1,)),
         )
         row_sq = jnp.concatenate([layer_sq[column * 2 + part] for part in parts], axis=1)
-        arg = (visitor_sq[layer] + row_sq - 2.0 * cross) * scale
+        arg = (visitor_sq[layer, begin : begin + count] + row_sq - 2.0 * cross) * scale
         value = jnp.exp(-jnp.maximum(arg, 0.0))
         product = four_products(
             jnp.concatenate(two_terms(value), axis=0),
@@ -165,7 +181,8 @@
             probes_low[where, :],
             ((1,), (0,)),
         )
-        sums[layer] = product if fresh else sums[layer] + product
+        kept = slice(begin, begin + count)
+        sums[layer, kept, :] = product if fresh else sums[layer, kept, :] + product
 
     barrier = pltpu.get_barrier_semaphore()
     for step in range(1, outer):
@@ -269,16 +286,19 @@
     take_rows(1)
     use_rows(1, near)
     for distance in range(1, near + 1):
-        both_ways(distance, lambda layer, way: back(layer).start())
-
-    def meet_all(layer, way):
-        meet_own(layer, way)
-        others(lambda step, column: pair(layer, column, (0, 1)))
-        back(layer).start()
+        for turn in range(2):
+            both_ways(distance, lambda layer, way, turn=turn: back(layer, turn).start())
+
+    def meet_all(layer, turn):
+        here = dict(begin=turn * (piece // 2), count=piece // 2)
+        prepare_visitor(layer, **here)
+        for column in range(0, inner, 2):
+            pair(layer, column, (0, 1, 2, 3), fresh=column == 0, **here)
+        back(layer, turn).start()
     for distance in range(near + 1, outer):
-        receive(distance, 0)
-        receive(distance, 1)
-        both_ways(distance, meet_all)
+        for turn in range(2):
+            receive(distance, turn)
+            both_ways(distance, lambda layer, way, turn=turn: meet_all(layer, turn))
 
     for way in (1, -1):
         @pl.when(inside(z + way))
@@ -301,11 +321,13 @@
     result = sums[z]
     for step in range(1, outer):
         layer = lax.rem(z + step, outer)
-        wait_recv(returned.at[layer], back_recv.at[layer])
+        for turn in range(2):
+            wait_recv(returned.at[layer, pl.ds(turn * (piece // 2), piece // 2)], back_recv.at[layer, turn])
         result = result + returned[layer]
     out_ref[...] = result
     for step in range(1, outer):
-        back(lax.rem(z + step, outer)).wait_send()
+        for turn in range(2):
+            back(lax.rem(z + step, outer), turn).wait_send()
 
 
 def body(points, probes):
@@ -341,8 +363,8 @@
             dma((inner - 1, 2, 2)),
             dma((inner - 1, 2, 2)),
             dma((inner * 4, 2)),
-            dma((outer,)),
-            dma((outer,)),
+            dma((outer, 2)),
+            dma((outer, 2)),
         ],
         compiler_params=pltpu.CompilerParams(collective_id=0, has_side_effects=True),
     )(points, probes)

time: 33.6 us -> 33.7 us (level)
  no operation moved by 1% of the time
where the time goes in v4:
time: 33.7 us; the launch traced here: 33.4 us
  Pallas kernels  31.9 us (95%)
  local copies, waits for them, and re-layouts  1.47 us (4%)
    pallas_call x1, Pallas kernels, body(): pl.pallas_call(functools.partial(kernel, outer, inner), out_shape=jax.Sha...  31.9 us
    unnamed x1, local copies, waits for them, and re-layouts  1.47 us

profile of v4, /device:TPU:0, one launch (start us, length us, event | category | flops | bytes accessed | tf_op | source)
XLA Modules:
  0.0 33.4 jit_solution(13217951412371070704)
XLA Ops:
  0.0 31.9 %shard_map.28 = f32[64,256]{1,0:T(8,128)} custom-call(f32[256,1024]{1,0:T(8,128)} %points_hbm.1, f32[256,256]{1,0:T(8,128)} %probes_hbm.1), custom_call_target="tpu_custom_call" | custom-call | tf_op jit(solution)/shard_map/pallas_call | solution.py:342
  31.9 1.5 %copy.4 = f32[64,256]{1,0:T(8,128)} copy(f32[64,256]{1,0:T(8,128)} %shard_map.28) | data formatting | bytes 131072

commit v5 on v4

--- a/solution.py
+++ b/solution.py
@@ -260,6 +260,11 @@
                 @pl.when(inside(layer))
                 def _():
                     pair(layer, column, (part,))
+                    if part == 1:
+                        @pl.when((layer != z) & (step == inner - 1))
+                        def _():
+                            back(layer, 0).start()
+                            back(layer, 1).start()
                 return carry
             lax.fori_loop(0, 2 * reach + 1, one, 0)
         others(use)
@@ -285,9 +290,6 @@
         both_ways(2, meet_more)
     take_rows(1)
     use_rows(1, near)
-    for distance in range(1, near + 1):
-        for turn in range(2):
-            both_ways(distance, lambda layer, way, turn=turn: back(layer, turn).start())
 
     def meet_all(layer, turn):
         here = dict(begin=turn * (piece // 2), count=piece // 2)

time: 33.7 us -> 31.9 us (0.947)
  Pallas kernels: 31.9 us -> 30.3 us
    pallas_call x1, Pallas kernels: 31.9 us -> 30.3 us  [body(): pl.pallas_call(functools.partial(kernel, outer, inner), out_shape=jax.Sha...]
where the time goes in v5:
time: 31.9 us; the launch traced here: 31.8 us
  Pallas kernels  30.3 us (95%)
  local copies, waits for them, and re-layouts  1.47 us (5%)
    pallas_call x1, Pallas kernels, body(): pl.pallas_call(functools.partial(kernel, outer, inner), out_shape=jax.Sha...  30.3 us
    unnamed x1, local copies, waits for them, and re-layouts  1.47 us

profile of v5, /device:TPU:0, one launch (start us, length us, event | category | flops | bytes accessed | tf_op | source)
XLA Modules:
  0.0 31.8 jit_solution(17978116131842548935)
XLA Ops:
  0.0 30.3 %shard_map.28 = f32[64,256]{1,0:T(8,128)} custom-call(f32[256,1024]{1,0:T(8,128)} %points_hbm.1, f32[256,256]{1,0:T(8,128)} %probes_hbm.1), custom_call_target="tpu_custom_call" | custom-call | tf_op jit(solution)/shard_map/pallas_call | solution.py:344
  30.3 1.5 %copy.4 = f32[64,256]{1,0:T(8,128)} copy(f32[64,256]{1,0:T(8,128)} %shard_map.28) | data formatting | bytes 131072
